TPU v7x, 32 devices: a whole 2x2x4 slice. The times are simulated.
32 devices in a mesh: azim: 8 (over z, x), frame: 4 (over y, core).
Axes of the slice: x: 2, y: 2, z: 4, core: 2. Of those that a mesh axis runs over, the one named last changes fastest.
Arguments:
- features: bfloat16 [4, 14, 112, 384], P('frame', None, 'azim'), may hold values from -6 to 6
- position_bias: float32 [169, 12], replicated, may hold values from -4 to 4
- attend_weight: bfloat16 [384, 1152], replicated, may hold values from -0.3125 to 0.3125
- output_weight: bfloat16 [384, 384], replicated, may hold values from -0.3125 to 0.3125
- merge_weight: bfloat16 [1536, 768], replicated, may hold values from -0.15625 to 0.15625
- cotangent: bfloat16 [4, 7, 56, 768], P('frame', None, 'azim'), may hold values from -6 to 6
Outputs:
- merged: bfloat16 [4, 7, 56, 768], P('frame', None, 'azim')
- feature_grad: bfloat16 [4, 14, 112, 384], P('frame', None, 'azim')
- attend_grad: float32 [442368], P(('azim', 'frame'))
- output_grad: float32 [147456], P(('azim', 'frame'))
All inputs are finite; a program needn't handle non-finite values.
Results may differ from a plain program's by a relative error of at most 0.0094.
Values may be sent and summed in bfloat16 or wider, within the bound.
No kernel may reach another device: no remote copies, remote signals or barrier semaphores. Data moves between devices by JAX's collectives and lax.ppermute only.
A program may use at most 64 MiB of HBM per device.

v0:
```python
import functools

import jax
import jax.numpy as jnp
import numpy as np
from jax import lax
from jax.experimental import pallas as pl
from jax.experimental.pallas import tpu as pltpu
from jax.sharding import PartitionSpec as P


WINDOW = 7
SHIFT = 3
SLOT = 64
LANES = 128
EPS = 1e-05


def up(value, step):
    return -(-value // step) * step


def dot(left, right):
    return lax.dot_general(left, right, (((1,), (0,)), ((), ())), preferred_element_type=jnp.float32)


def dot_t(left, right):
    return lax.dot_general(left, right, (((1,), (1,)), ((), ())), preferred_element_type=jnp.float32)


def pick(select, values):
    return dot(select, values).astype(jnp.bfloat16)


class Grid:
    def __init__(self, rows, cols, heads, channels):
        self.rows, self.cols, self.heads, self.channels = rows, cols, heads, channels
        self.west = WINDOW - SHIFT
        self.last = cols - self.west
        self.bands, self.across = rows // WINDOW, cols // WINDOW
        self.windows = self.bands * self.across
        self.local_windows = self.windows - self.bands
        self.window_rows, self.local_rows = self.windows * SLOT, self.local_windows * SLOT
        self.stride = up(cols, 16)
        self.own_rows = rows * self.stride
        self.west_rows = up(rows * self.west, 16)
        self.quad_lines, self.quad_cols, self.quad_west = rows // 2, cols // 2, self.west // 2
        self.quad_stride = up(self.quad_cols, 8)
        self.quad_count = up(self.quad_lines * self.quad_stride, 16)
        self.cot_stride = up(self.quad_cols, 16)
        self.cot_own = self.quad_lines * self.cot_stride
        self.cot_halo = up(self.quad_west * self.quad_lines, 16)

    def source(self, row, col):
        return row * self.stride + col if col >= 0 else self.own_rows + row * self.west + col + self.west

    def window_row(self, row, col):
        line = (row - SHIFT) % self.rows
        across, place = divmod(col + self.west, WINDOW)
        window = (across - 1) % self.across * self.bands + line // WINDOW
        return window * SLOT + line % WINDOW * (WINDOW + 1) + place

    def quad_row(self, row, col):
        phase = 2 * (col % 2) + row % 2
        return phase * self.quad_count + row // 2 * self.quad_stride + (col + self.west) // 2

    def onehot(self, shape, pairs):
        out = np.zeros(shape, np.float32)
        for i, j in pairs:
            out[i, j] = 1
        return jnp.asarray(out, jnp.bfloat16)

    def cells(self, first, last):
        return [(r, c) for r in range(self.rows) for c in range(first, last)]

    def to_windows(self):
        pairs = [(self.window_row(r, c), self.source(r, c)) for r, c in self.cells(-self.west, self.last)]
        return self.onehot((self.window_rows, self.own_rows + self.west_rows), pairs)

    def to_quads(self):
        pairs = [(self.quad_row(r, c), self.window_row(r, c)) for r, c in self.cells(-self.west, self.last)]
        return self.onehot((4 * self.quad_count, self.window_rows), pairs)

    def from_quads(self):
        return self.to_quads().T

    def pack_tokens(self):
        pairs = [
            (r * self.west + c - self.last, self.source(r, c)) for r, c in self.cells(self.last, self.cols)
        ]
        return self.onehot((self.west_rows, self.own_rows), pairs)

    def quad_cells(self, first, last):
        return [(i, j) for i in range(self.quad_lines) for j in range(first, last)]

    def pack_cot(self):
        first = self.quad_cols - self.quad_west
        pairs = [
            (self.quad_west * i + j - first, i * self.cot_stride + j)
            for i, j in self.quad_cells(first, self.quad_cols)
        ]
        return self.onehot((self.cot_halo, self.cot_own), pairs)

    def cot_to_quads(self):
        pairs = [
            (i * self.quad_stride + j, self.cot_own + self.quad_west * i + j)
            for i, j in self.quad_cells(0, self.quad_west)
        ]
        pairs += [
            (i * self.quad_stride + j, i * self.cot_stride + j - self.quad_west)
            for i, j in self.quad_cells(self.quad_west, self.quad_cols)
        ]
        return self.onehot((self.quad_count, self.cot_own + self.cot_halo), pairs)

    def tokens_back(self):
        pairs = [(r * self.west + c + self.west, self.window_row(r, c)) for r, c in self.cells(-self.west, 0)]
        return self.onehot((self.west_rows, self.window_rows), pairs)

    def quads_back(self):
        pairs = [
            (self.quad_west * i + j, i * self.quad_stride + j) for i, j in self.quad_cells(0, self.quad_west)
        ]
        return self.onehot((self.cot_halo, self.quad_count), pairs)

    def final_tokens(self):
        pairs = [(self.source(r, c), self.window_row(r, c)) for r, c in self.cells(0, self.last)]
        pairs += [
            (self.source(r, c), self.window_rows + r * self.west + c - self.last)
            for r, c in self.cells(self.last, self.cols)
        ]
        return self.onehot((self.own_rows, self.window_rows + self.west_rows), pairs)

    def final_quads(self):
        first = self.quad_cols - self.quad_west
        pairs = [
            (i * self.quad_stride + j, i * self.quad_stride + j + self.quad_west)
            for i, j in self.quad_cells(0, first)
        ]
        pairs += [
            (i * self.quad_stride + j, self.quad_count + self.quad_west * i + j - first)
            for i, j in self.quad_cells(first, self.quad_cols)
        ]
        return self.onehot((self.quad_count, self.quad_count + self.cot_halo), pairs)


def normalize(values):
    centred = values - jnp.mean(values, -1, keepdims=True)
    inverse_std = lax.rsqrt(jnp.mean(centred * centred, -1, keepdims=True) + EPS)
    return centred * inverse_std, inverse_std


def spread(ref, grid_ref, stride):
    ref[0 : grid_ref.shape[0] * stride, :] = jnp.zeros((grid_ref.shape[0] * stride, ref.shape[1]), ref.dtype)
    for line in range(grid_ref.shape[0]):
        ref[line * stride : line * stride + grid_ref.shape[1], :] = grid_ref[line]


def pack(grid, out, tokens, quads):
    out[0 : grid.west_rows, :] = tokens
    for part in range(quads.shape[1] // grid.channels):
        first = grid.west_rows + part * grid.cot_halo
        out[first : first + grid.cot_halo, :] = quads[:, part * grid.channels : (part + 1) * grid.channels]


def unpack(grid, ref, width):
    first = grid.west_rows
    parts = [
        ref[first + part * grid.cot_halo : first + (part + 1) * grid.cot_halo, :]
        for part in range(width // grid.channels)
    ]
    return ref[0 : grid.west_rows, :], jnp.concatenate(parts, 1)


def pre_kernel(grid, x, cot, pack_tokens, pack_cot, to_next, tokens, quads):
    spread(tokens, x.get(), grid.stride)
    spread(quads, cot.get(), grid.cot_stride)
    halo = pick(pack_cot.get()[...], quads[...])
    pack(grid, to_next.ref, pick(pack_tokens.get()[...], tokens[...]), halo)
    to_next.send()


def build_bias(grid, table, bias, mask):
    span, count = 2 * WINDOW - 1, WINDOW + 1
    per_group = LANES * grid.heads // grid.channels
    center = (WINDOW - 1) * span + WINDOW - 1
    rows = table.shape[1]
    values = jnp.concatenate([table[...], jnp.zeros((table.shape[0], 2 * LANES - rows), jnp.float32)], 1)
    key = lax.broadcasted_iota(jnp.int32, (SLOT, per_group * SLOT), 0)
    query = lax.broadcasted_iota(jnp.int32, (SLOT, per_group * SLOT), 1) & (SLOT - 1)
    key_row, key_col = key >> 3, key & (count - 1)
    query_row = query >> 3
    padded = jnp.where((key_row < WINDOW) & (key_col < WINDOW), 0.0, -1e30)
    key_late = (key_row >= WINDOW - SHIFT).astype(jnp.int32)
    query_late = (query_row >= WINDOW - SHIFT).astype(jnp.int32)
    mask[...] = jnp.where(key_late != query_late, -100.0, 0.0)
    place = lax.broadcasted_iota(jnp.int32, (LANES, per_group * SLOT), 0)
    lane = lax.broadcasted_iota(jnp.int32, (LANES, per_group * SLOT), 1)
    inside = lane & (SLOT - 1)
    wanted = (inside >> 3) * span + (inside & (count - 1))
    hit = (place == wanted) & ((inside >> 3) < WINDOW) & ((inside & (count - 1)) < WINDOW)
    for group in range(grid.heads // per_group):
        total = padded
        for head in range(per_group):
            line = jnp.broadcast_to(values[group * per_group + head : group * per_group + head + 1], (count, 2 * LANES))
            line = pltpu.roll(line, 0, 1, stride=1, stride_axis=0)
            blocks = [
                pltpu.roll(line, (span * r - center) % (2 * LANES), 1)[:, :LANES] for r in range(WINDOW)
            ]
            blocks.append(jnp.zeros((count, LANES), jnp.float32))
            block = jnp.concatenate(blocks, 0)
            high = block.astype(jnp.bfloat16)
            low = (block - high.astype(jnp.float32)).astype(jnp.bfloat16)
            select = jnp.where(hit & ((lane // SLOT) == head), 1.0, 0.0).astype(jnp.bfloat16)
            total = total + dot(high, select) + dot(low, select)
        bias[group] = total


class Heads:
    def __init__(self, grid, head_mask):
        self.channels = grid.channels
        self.head_size = grid.channels // grid.heads
        self.scale = self.head_size ** (-0.5)
        self.per_group = LANES // self.head_size
        self.groups = grid.heads // self.per_group
        self.head_mask = head_mask

    def spread(self, values):
        return jnp.concatenate([values] * self.per_group, 0) * self.head_mask

    def collect(self, stacked):
        total = None
        for head in range(self.per_group):
            part = stacked[head * SLOT : (head + 1) * SLOT, :]
            part = jnp.where(self.head_mask[head * SLOT : (head + 1) * SLOT, :] > 0, part, 0.0)
            total = part if total is None else total + part
        return total

    def split(self, projected, window, group):
        rows = slice(window * SLOT, (window + 1) * SLOT)
        firsts = [part * self.channels + group * LANES for part in range(3)]
        return [projected[rows, first : first + LANES] for first in firsts]

    def forward(self, jobs, fillers=()):
        def product(job):
            query, key, value = self.split(job.projected, job.window, job.group)
            return dot_t(key, self.spread(query)), value

        def soften(job, scores, value):
            scores = scores * self.scale + job.bias[job.group]
            if job.extra is not None:
                scores = scores + job.extra[...]
            weights = jnp.exp(scores - jnp.max(scores, 0, keepdims=True))
            prob = weights / jnp.sum(weights, 0, keepdims=True)
            job.probs[job.window * self.groups + job.group] = prob
            return prob.astype(jnp.bfloat16), value

        def mix(job, prob, value):
            return (dot(prob.T, value),)

        def store(job, mixed):
            rows, lanes = job.window * SLOT, job.group * LANES
            job.attended[rows : rows + SLOT, lanes : lanes + LANES] = self.collect(mixed).astype(jnp.bfloat16)
            return ()

        interleave(jobs, (product, soften, mix, store), fillers)

    def backward(self, jobs, outer, projected_grad, fillers=()):
        def rows_of(job):
            return slice(job.first + job.window * SLOT, job.first + (job.window + 1) * SLOT)

        def put(job, part, grad):
            at = part * self.channels + job.group * LANES
            projected_grad[rows_of(job), at : at + LANES] = grad.astype(jnp.bfloat16)

        def product(job):
            value = self.split(job.projected, job.window, job.group)[2]
            grads = self.spread(outer[rows_of(job), job.group * LANES : (job.group + 1) * LANES])
            prob = job.probs[job.window * self.groups + job.group]
            put(job, 2, dot(prob.astype(jnp.bfloat16), grads))
            return (dot_t(value, grads),)

        def soften(job, score_grad):
            prob = job.probs[job.window * self.groups + job.group]
            inner = jnp.sum(prob * score_grad, 0, keepdims=True)
            return ((prob * (score_grad - inner) * self.scale).astype(jnp.bfloat16),)

        def mix(job, soft):
            query, key, _ = self.split(job.projected, job.window, job.group)
            put(job, 1, dot(soft, self.spread(query)))
            return (dot(soft.T, key),)

        def store(job, mixed):
            put(job, 0, self.collect(mixed))
            return ()

        interleave(jobs, (product, soften, mix, store), fillers)


class Job:
    def __init__(self, **fields):
        self.__dict__.update(fields)


def jobs_of(windows, groups, **fields):
    return [Job(window=window, group=group, **fields) for window in range(windows) for group in range(groups)]


def interleave(jobs, stages, fillers=()):
    states = [()] * len(jobs)
    fillers = list(fillers)
    for turn in range(len(jobs) + len(stages) - 1):
        for depth, stage in reversed(list(enumerate(stages))):
            at = turn - depth
            if 0 <= at < len(jobs):
                states[at] = stage(jobs[at], *states[at])
        if fillers:
            fillers.pop(0)()
    for filler in fillers:
        filler()


def with_masks(jobs, grid, mask):
    for job in jobs:
        job.extra = mask if job.window % grid.bands == grid.bands - 1 else None
    return jobs


def local_kernel(grid, x, cot, table, to_windows, attend_weight, head_mask, *rest):
    tokens = rest[-1]
    bias, mask, quads, windowed, normed, std, projected, attended, probs, orders, rolled_t, attended_t = [
        r.ref for r in rest[-13:-1]
    ]
    spread(quads, cot.get(), grid.cot_stride)
    spread(tokens, x.get(), grid.stride)
    build_bias(grid, table.get(), bias, mask)
    values = dot(to_windows.get()[:, : grid.own_rows], tokens[...])
    windowed[...] = values
    local = grid.local_rows
    n, inverse_std = normalize(values[:local])
    normed[...] = n
    std[...] = inverse_std
    projected[...] = dot(n.astype(jnp.bfloat16), attend_weight.get()[...]).astype(jnp.bfloat16)
    heads = Heads(grid, head_mask.get()[...])
    jobs = jobs_of(
        grid.local_windows, heads.groups, projected=projected, bias=bias, attended=attended, probs=probs
    )
    heads.forward(with_masks(jobs, grid, mask))
    rolled = n.astype(jnp.bfloat16)
    order = row_order(grid.channels)
    orders[...] = order
    rolled_t[...] = dot_t(order, rolled).astype(jnp.bfloat16)
    attended_t[...] = dot_t(order, attended[...]).astype(jnp.bfloat16)


def main_kernel(
    grid, from_west, to_windows, attend_weight, head_mask, bias, mask, to_quads, output_weight,
    cot_to_quads, merge_weight, from_quads, quads, windowed_own, normed_local, std_local, projected_local,
    attended_local, probs_local, orders, rolled_t_local, attended_t_local,
    kept, sent, projected_grad_out, normed_out, std_out, branch_grad_out, quad16_out,
    projected, attended, probs, outer, quad_grads, rolled_t, attended_t,
):
    channels, local = grid.channels, grid.local_rows
    west_tokens, west_quads = unpack(grid, from_west.get(), quads.ref.shape[1])
    windowed = windowed_own.ref[...] + dot(to_windows.ref[:, grid.own_rows :], west_tokens)
    normed, inverse_std = normalize(windowed[local:])
    normed_out.ref[:local] = normed_local.ref[...]
    normed_out.ref[local:] = normed
    std_out.ref[:local] = std_local.ref[...]
    std_out.ref[local:] = inverse_std
    projected[...] = dot(normed.astype(jnp.bfloat16), attend_weight.ref[...]).astype(jnp.bfloat16)
    rolled = normed.astype(jnp.bfloat16)
    cot_select = cot_to_quads.ref
    cot_quads = dot(cot_select[:, : grid.cot_own], quads.ref[: grid.cot_own, :])
    cot_quads = (cot_quads + dot(cot_select[:, grid.cot_own :], west_quads)).astype(jnp.bfloat16)
    merge_ref = merge_weight.ref

    def quad_product(k):
        quad_grads[k] = dot_t(cot_quads, merge_ref[k * channels : (k + 1) * channels, :])

    heads = Heads(grid, head_mask.ref[...])
    jobs = jobs_of(grid.bands, heads.groups, projected=projected, bias=bias.ref, attended=attended, probs=probs)
    heads.forward(
        with_masks(jobs, grid, mask.ref), [functools.partial(quad_product, k) for k in range(4)]
    )

    select = to_quads.ref
    attended_quads = (
        dot(select[:, :local], attended_local.ref[...]) + dot(select[:, local:], attended[...])
    ).astype(jnp.bfloat16)
    feature_quads = dot(select[...], windowed.astype(jnp.bfloat16))
    branch = dot(attended_quads, output_weight.ref[...])
    hidden = (feature_quads + branch).astype(jnp.bfloat16).astype(jnp.float32)
    count = grid.quad_count
    phases = [hidden[k * count : (k + 1) * count] for k in range(4)]
    width = 4 * channels
    mean = sum(jnp.sum(phase, -1, keepdims=True) for phase in phases) / width
    centred = [phase - mean for phase in phases]
    variance = sum(jnp.sum(phase * phase, -1, keepdims=True) for phase in centred) / width
    quad_std = lax.rsqrt(variance + EPS)
    quad_normed = [phase * quad_std for phase in centred]
    for k in range(4):
        quad16_out.ref[k * count : (k + 1) * count, :] = quad_normed[k].astype(jnp.bfloat16)
    first = sum(jnp.sum(quad_grads[k], -1, keepdims=True) for k in range(4)) / width
    second = sum(jnp.sum(quad_grads[k] * quad_normed[k], -1, keepdims=True) for k in range(4)) / width
    hidden_grad = jnp.concatenate(
        [quad_std * (quad_grads[k] - first - quad_normed[k] * second) for k in range(4)], 0
    ).astype(jnp.bfloat16)
    branch_grad = pick(from_quads.ref[...], hidden_grad)
    branch_grad_out.ref[...] = branch_grad
    outer[...] = dot_t(branch_grad, output_weight.ref[...]).astype(jnp.bfloat16)
    projected_grad = projected_grad_out.ref
    jobs = jobs_of(
        grid.local_windows, heads.groups, projected=projected_local.ref, probs=probs_local.ref, first=0
    )
    jobs += jobs_of(grid.bands, heads.groups, projected=projected, probs=probs, first=local)

    def turned():
        rolled_t[...] = dot_t(orders.ref[...], rolled).astype(jnp.bfloat16)

    def turned_attended():
        attended_t[...] = dot_t(orders.ref[...], attended[...]).astype(jnp.bfloat16)

    heads.backward(jobs, outer, projected_grad, [turned_attended, turned])

    half, joint = channels // 2, 3 * channels

    def put(first, local_t, halo_t, grads):
        piece = dot(local_t, grads[:local]) + dot(halo_t, grads[local:])
        kept.ref[:, first : first + piece.shape[1]] = piece[:half]
        sent.ref[:, first : first + piece.shape[1]] = piece[half:].astype(jnp.bfloat16)

    put(joint, attended_t_local.ref[...], attended_t[...], branch_grad)
    for first in range(0, joint, channels):
        put(first, rolled_t_local.ref[...], rolled_t[...], projected_grad[:, first : first + channels])


def tail_kernel(
    grid, projected_grad, attend_weight, normed, inverse_std, branch_grad, quads_back, tokens_back, merged,
    back, feature_grads,
):
    grads = dot_t(projected_grad.get()[...], attend_weight.get()[...])
    n = normed.get()[...]
    first = jnp.mean(grads, -1, keepdims=True)
    second = jnp.mean(grads * n, -1, keepdims=True)
    rolled_grad = inverse_std.get()[...] * (grads - first - n * second)
    total = (branch_grad.get()[...].astype(jnp.float32) + rolled_grad).astype(jnp.bfloat16)
    feature_grads.ref[...] = total
    feature_grads.send()
    pack(grid, back.ref, pick(tokens_back.get()[...], total), pick(quads_back.get()[...], merged.get()[...]))
    back.send()


def merge_kernel(grid, quad16, merge_weight, merged):
    channels, count = grid.channels, grid.quad_count
    sums = None
    quad_ref, merge_ref = quad16.get(), merge_weight.get()
    for k in range(4):
        term = dot(quad_ref[k * count : (k + 1) * count, :], merge_ref[k * channels : (k + 1) * channels, :])
        sums = term if sums is None else sums + term
    merged.ref[...] = sums.astype(jnp.bfloat16)
    merged.send()


def last_kernel(grid, feature_grads, merged, came, final_tokens, final_quads, out, merged_out):
    width = merged_out.ref.shape[2]
    tokens, quads = unpack(grid, came.get(), width)
    rows = grid.window_rows
    select = final_tokens.get()
    total = dot(select[:, :rows], feature_grads.get()[...]) + dot(select[:, rows:], tokens)
    for line in range(grid.rows):
        out.ref[line] = total[line * grid.stride : line * grid.stride + grid.cols].astype(jnp.bfloat16)
    out.send()
    select = final_quads.get()
    count = grid.quad_count
    sums = dot(select[:, :count], merged.get()[...]) + dot(select[:, count:], quads)
    for line in range(grid.quad_lines):
        first = line * grid.quad_stride
        merged_out.ref[line] = sums[first : first + grid.quad_cols].astype(jnp.bfloat16)
    merged_out.send()


class Operand:
    def __init__(self, source, ref, sem):
        self.ref, self.copy, self.waited = ref, pltpu.make_async_copy(source, ref, sem), False
        self.copy.start()

    def get(self):
        if not self.waited:
            self.copy.wait()
            self.waited = True
        return self.ref


class Result:
    def __init__(self, target, ref, sem):
        self.ref, self.copy = ref, pltpu.make_async_copy(ref, target, sem)

    def send(self):
        self.copy.start()

    def wait(self):
        self.copy.wait()


class Held:
    def __init__(self, array):
        self.array = array


class Load:
    def __init__(self, array):
        self.array = array


class HeldRef:
    def __init__(self, ref):
        self.ref = ref

    def get(self):
        return self.ref

    def send(self):
        pass

    def wait(self):
        pass


def call(kernel, outs, *args, scratch=()):
    given = [getattr(arg, "array", arg) for arg in args]
    loads = [arg.array for arg in args if isinstance(arg, Load)]
    made = [*[Held(load) for load in loads], *outs]
    plain = [arg for arg in args if not isinstance(arg, (Held, Load))]
    plain += [out for out in outs if not isinstance(out, Held)]

    def body(*refs):
        refs = list(refs)
        ins, refs = refs[: len(given)], refs[len(given) :]
        loaded, refs = refs[: len(loads)], refs[len(loads) :]
        results, refs = refs[: len(outs)], refs[len(outs) :]
        inner, refs = refs[: len(scratch)], refs[len(scratch) :]
        buffers, sems = refs[:-1], refs[-1]
        count = 0
        operands = []
        for arg, ref in zip(args, ins):
            if isinstance(arg, Held):
                operands.append(HeldRef(ref))
                continue
            target = loaded.pop(0) if isinstance(arg, Load) else buffers.pop(0)
            operands.append(Operand(ref, target, sems.at[count]))
            count += 1
        outputs = []
        for out, ref in zip(outs, results):
            if isinstance(out, Held):
                outputs.append(HeldRef(ref))
                continue
            outputs.append(Result(ref, buffers.pop(0), sems.at[count]))
            count += 1
        kernel(*operands, *outputs, *inner)
        for operand in operands:
            operand.get()
        for output in outputs:
            output.wait()

    def space(item):
        return pltpu.VMEM if isinstance(item, Held) else pltpu.HBM

    results = pl.pallas_call(
        body,
        out_shape=[space(m)(getattr(m, "array", m).shape, getattr(m, "array", m).dtype) for m in made],
        in_specs=[pl.BlockSpec(memory_space=space(arg)) for arg in args],
        out_specs=[pl.BlockSpec(memory_space=space(m)) for m in made],
        scratch_shapes=[
            *scratch,
            *[pltpu.VMEM(a.shape, a.dtype) for a in plain],
            pltpu.SemaphoreType.DMA((max(len(plain) + len(loads), 1),)),
        ],
        compiler_params=pltpu.CompilerParams(vmem_limit_bytes=24 * 2**20),
    )(*[pltpu.with_memory_space_constraint(a, space(arg)) for a, arg in zip(given, args)])
    return [Held(result) if isinstance(m, Held) else result for result, m in zip(results, made)]


def f32(*shape):
    return jax.ShapeDtypeStruct(shape, jnp.float32)


def b16(*shape):
    return jax.ShapeDtypeStruct(shape, jnp.bfloat16)


def held(shape):
    return Held(shape)


def bit_groups():
    frame_bits = lax.axis_size("frame").bit_length() - 1
    azim_bits = lax.axis_size("azim").bit_length() - 1
    frame = [1 << bit for bit in range(frame_bits)]
    azim = [1 << (bit + frame_bits) for bit in range(azim_bits)]
    return [frame[:1], azim[:1] + frame[1:2], azim[:0:-1] + frame[:1:-1]]


def exchange(block, mask):
    members = lax.axis_size(("azim", "frame"))
    return lax.ppermute(block, ("azim", "frame"), [(i, i ^ mask) for i in range(members)])


def row_order(channels):
    row = lax.broadcasted_iota(jnp.int32, (channels, channels), 0)
    column = lax.broadcasted_iota(jnp.int32, (channels, channels), 1)
    weights = sum(bit_groups(), [])
    members = 1 << len(weights)
    if channels % members == 0:
        each = channels // members
        me = lax.axis_index("azim") * lax.axis_size("frame") + lax.axis_index("frame")
        part = jnp.floor((row.astype(jnp.float32) + 0.5) * (1.0 / each)).astype(jnp.int32)
        row = row - part * each
        for stage, weight in enumerate(weights):
            far = (part >> (len(weights) - 1 - stage)) & 1
            own = (me >> (weight.bit_length() - 1)) & 1
            row = row + (far ^ own) * (weight * each)
    return jnp.where(column == row, 1.0, 0.0).astype(jnp.bfloat16)


def scatter_flat(terms):
    weights = sum(bit_groups(), [])
    members = 1 << len(weights)
    widths = [term.size // members for term in terms]
    held = jnp.concatenate([term.reshape(members, -1) for term in terms], 1).astype(jnp.bfloat16)
    held = held.reshape((2,) * len(weights) + (-1,))
    me = lax.axis_index(("azim", "frame"))
    for weight in weights:
        dim = len(weights) - weight.bit_length()
        own = (me >> (weight.bit_length() - 1)) & 1
        kept = lax.dynamic_slice_in_dim(held, own, 1, dim)
        got = exchange(lax.dynamic_slice_in_dim(held, 1 - own, 1, dim), weight)
        total = kept.astype(jnp.float32) + got.astype(jnp.float32)
        held = total.astype(jnp.bfloat16)
    total = total.reshape(-1)
    return total[: widths[0]], total[widths[0] :]


def swap(total, weights):
    count = 1 << len(weights)
    rows = total.shape[0] // count
    gots = []
    for block in range(count - 1, 0, -1):
        mask = sum(w for i, w in enumerate(weights) if block >> (len(weights) - 1 - i) & 1)
        part = total[block * rows : (block + 1) * rows].astype(jnp.bfloat16)
        gots.append(exchange(part, mask))
    return gots


def finish_kernel(split, total, *rest):
    gots, (attend_grad, output_grad) = rest[:-2], rest[-2:]
    rows = gots[0].ref.shape[0]
    sums = total.get()[:rows, :]
    for got in gots:
        sums = sums + got.get()[...].astype(jnp.float32)
    for out, first, last in ((attend_grad, 0, split), (output_grad, split, sums.shape[1])):
        tiles = (last - first) // LANES
        for tile in range(tiles):
            at = first + tile * LANES
            out.ref[pl.ds(tile, rows, stride=tiles), :] = sums[:, at : at + LANES]
        out.send()


def scatter_sum(kept, sent, channels):
    groups = bit_groups()
    split = 3 * channels
    if channels % (1 << len(sum(groups, []))):
        whole = jnp.concatenate([kept, sent.astype(jnp.float32)], 0)
        return scatter_flat((whole[:, :split], whole[:, split:]))
    total = kept + exchange(sent, groups[0][0]).astype(jnp.float32)
    gots = swap(total, groups[1])
    total = sum((got.astype(jnp.float32) for got in gots), total[: gots[0].shape[0]])
    gots = swap(total, groups[2])
    rows = gots[0].shape[0]
    attend_grad, output_grad = call(
        functools.partial(finish_kernel, split),
        (f32(rows * split // LANES, LANES), f32(rows * channels // LANES, LANES)),
        Held(total), *[Held(got) for got in gots],
    )
    return attend_grad.reshape(-1), output_grad.reshape(-1)


def from_behind(block, axis, distance):
    size = lax.axis_size(axis)
    return lax.ppermute(block, axis, [((i - distance) % size, i) for i in range(size)])


def per_device(features, position_bias, attend_weight, output_weight, merge_weight, cotangent):
    x, cot = features[0], cotangent[0]
    rows, cols, channels = x.shape
    heads = position_bias.shape[1]
    grid = Grid(rows, cols, heads, channels)
    width = cot.shape[2]
    bf16 = jnp.bfloat16
    halo_rows = grid.west_rows + width // channels * grid.cot_halo
    own, local, quads = grid.window_rows, grid.local_rows, 4 * grid.quad_count
    per_group = LANES * heads // channels
    groups, across = heads // per_group, per_group * SLOT
    lane_head = np.arange(LANES) // (channels // heads)
    head_mask = jnp.asarray(np.repeat(np.arange(per_group), SLOT)[:, None] == lane_head[None, :]).astype(bf16)
    (to_next,) = call(
        functools.partial(pre_kernel, grid), (held(b16(halo_rows, channels)),),
        x, cot, grid.pack_tokens(), grid.pack_cot(),
        scratch=[pltpu.VMEM((grid.own_rows, channels), bf16), pltpu.VMEM((grid.cot_own, width), bf16)],
    )
    from_west = Held(from_behind(to_next.array, "azim", 1))
    halo = grid.bands * SLOT
    (
        to_windows, attend_held, mask_held, merge_held, output_held, to_quads, cot_to_quads, from_quads, quads_back,
        tokens_back, final_tokens, final_quads, bias, mask, quad_tokens, windowed, normed_local, std_local,
        projected, attended, probs, orders, rolled_t, attended_t,
    ) = call(
        functools.partial(local_kernel, grid),
        (
            held(f32(groups, SLOT, across)), held(f32(SLOT, across)), held(b16(grid.cot_own, width)),
            held(f32(own, channels)), held(f32(local, channels)), held(f32(local, 1)),
            held(b16(local, 3 * channels)), held(b16(local, channels)),
            held(f32(grid.local_windows * groups, SLOT, across)),
            held(b16(channels, channels)),
            held(b16(channels, local)), held(b16(channels, local)),
        ),
        x, cot, position_bias.T, Load(grid.to_windows()), Load(attend_weight), Load(head_mask), Load(merge_weight),
        Load(output_weight), Load(grid.to_quads()), Load(grid.cot_to_quads()), Load(grid.from_quads()),
        Load(grid.quads_back()), Load(grid.tokens_back()), Load(grid.final_tokens()), Load(grid.final_quads()),
        scratch=[pltpu.VMEM((grid.own_rows, channels), bf16)],
    )
    half = channels // 2
    kept, sent, projected_grad, normed, inverse_std, branch_grad, quad16 = call(
        functools.partial(main_kernel, grid),
        (
            held(f32(half, 4 * channels)), held(b16(half, 4 * channels)), held(b16(own, 3 * channels)),
            held(f32(own, channels)), held(f32(own, 1)), held(b16(own, channels)), held(b16(quads, channels)),
        ),
        from_west, to_windows, attend_held, mask_held, bias, mask, to_quads, output_held, cot_to_quads, merge_held,
        from_quads, quad_tokens, windowed, normed_local, std_local, projected, attended, probs, orders,
        rolled_t, attended_t,
        scratch=[
            pltpu.VMEM((halo, 3 * channels), bf16),
            pltpu.VMEM((halo, channels), bf16),
            pltpu.VMEM((grid.bands * groups, SLOT, across), jnp.float32),
            pltpu.VMEM((own, channels), bf16),
            pltpu.VMEM((4, grid.quad_count, channels), jnp.float32),
            pltpu.VMEM((channels, halo), bf16),
            pltpu.VMEM((channels, halo), bf16),
        ],
    )
    (merged_quads,) = call(
        functools.partial(merge_kernel, grid), (held(b16(grid.quad_count, width)),), quad16, merge_held
    )
    back, feature_grads = call(
        functools.partial(tail_kernel, grid), (held(b16(halo_rows, channels)), held(b16(own, channels))),
        projected_grad, attend_held, normed, inverse_std, branch_grad, quads_back, tokens_back, merged_quads,
    )
    came = Held(from_behind(back.array, "azim", -1))
    feature_grad, merged = call(
        functools.partial(last_kernel, grid),
        (b16(rows, cols, channels), b16(grid.quad_lines, grid.quad_cols, width)),
        feature_grads, merged_quads, came, final_tokens, final_quads,
    )
    attend_grad, output_grad = scatter_sum(kept.array, sent.array, channels)
    return (merged[None], feature_grad[None], attend_grad, output_grad)


def solution(mesh):
    in_specs = (P("frame", None, "azim", None), P(), P(), P(), P(), P("frame", None, "azim", None))
    out_specs = (
        P("frame", None, "azim", None),
        P("frame", None, "azim", None),
        P(("azim", "frame")),
        P(("azim", "frame")),
    )

    return jax.shard_map(per_device, mesh=mesh, in_specs=in_specs, out_specs=out_specs, check_vma=False)
```

profile of v0, /device:TPU:0, one launch (start us, length us, event | category | flops | bytes accessed | tf_op | source)
XLA Modules:
  0.0 38.4 jit_solution(5876969908207287463)
XLA Ops:
  0.6 1.3 %shard_map.192 = bf16[96,384]{1,0:T(8,128)(2,1)S(1)} custom-call(bf16[14,14,384]{2,1,0:T(8,128)(2,1)} %bitcast.7, bf16[7,7,768]{2,1,0:T(8,128)(2,1)} %bitcast.9, bf16[64,224]{1,0:T(8,128)(2,1)} %constant.21.clone.refs_2_, bf16[16,112]{1,0:T(8,128)(2,1)} %constant.22.clone.refs_3_), custom_call_target="tpu_custom_call" | custom-call | tf_op jit(solution)/shard_map/pallas_call | solution.py:568
  2.0 3.0 %collective-permute-start = (bf16[96,384]{1,0:T(8,128)(2,1)S(1)}, bf16[96,384]{1,0:T(8,128)(2,1)S(1)}, u32[]{:S(2)}, u32[]{:S(2)}) collective-permute-start(bf16[96,384]{1,0:T(8,128)(2,1)S(1)} %shard_map.192), channel_id=1, source_target_pairs={{28,0},{0,4},{4,8},{8,12},{12,16},{16,20},{20,24},{24,28},{29,1},{... | collective-permute-start | bytes 221192 | tf_op jit(solution)/shard_map/ppermute | solution.py:689
  5.0 3.5 %shard_map.193 = (bf16[256,288]{1,0:T(8,128)(2,1)S(1)}, bf16[384,1152]{1,0:T(8,128)(2,1)S(1)}, bf16[256,128]{1,0:T(8,128)(2,1)S(1)}, bf16[1536,768]{1,0:T(8,128)...) custom-call(bf16[14,14,384]{2,1,0:T(8,128)(2,1)} %bitcast.8, ...), custom_call_target="tpu_custom_call" | custom-call | tf_op jit(solution)/shard_map/pallas_call | solution.py:568
  8.5 1.9 %collective-permute-done.refs_0_ = bf16[96,384]{1,0:T(8,128)(2,1)S(1)} collective-permute-done((bf16[96,384]{1,0:T(8,128)(2,1)S(1)}, bf16[96,384]{1,0:T(8,128)(2,1)S(1)}, u32[]{:S(2)}, u32[]{:S(2)}) %collective-permute-start) | collective-permute-done | bytes 73760 | tf_op jit(solution)/shard_map/ppermute | solution.py:689
  10.4 5.5 %shard_map.194 = (f32[192,1536]{1,0:T(8,128)S(1)}, bf16[192,1536]{1,0:T(8,128)(2,1)S(1)}, bf16[256,1152]{1,0:T(8,128)(2,1)S(1)}, f32[256,384]{1,0:T(8,128)S(1)},...) custom-call(bf16[96,384]{1,0:T(8,128)(2,1)S(1)} %collective-permute-done.refs_0_, ...), custom_call_target="tpu_custom_call" | custom-call | tf_op jit(solution)/shard_map/pallas_call | solution.py:568
  15.9 0.1 collective-permute-start.2
  16.0 2.0 %collective-permute-done.2 = bf16[192,1536]{1,0:T(8,128)(2,1)S(1)} collective-permute-done((bf16[192,1536]{1,0:T(8,128)(2,1)S(1)}, bf16[192,1536]{1,0:T(8,128)(2,1)S(1)}, u32[]{:S(2)}, u32[]{:S(2)}) %collective-permute-start.2) | collective-permute-done | bytes 589856 | tf_op jit(solution)/shard_map/ppermute | solution.py:605
  18.0 0.2 fusion.4
  18.2 0.7 %collective-permute-start.3 = (bf16[48,1536]{1,0:T(8,128)(2,1)S(1)}, bf16[48,1536]{1,0:T(8,128)(2,1)S(1)}, u32[]{:S(2)}, u32[]{:S(2)}) collective-permute-start(bf16[48,1536]{1,0:T(8,128)(2,1)S(1)} %get-tuple-element.82), channel_id=1, source_target_pairs={{0,6},{1,7},{2,4},{3,5},{4,2},{5,3},{6,0},{7,1},{8,14},{9,15},{10,... | collective-permute-start | bytes 442376 | tf_op jit(solution)/shard_map/ppermute | solution.py:605
  18.9 1.1 %collective-permute-start.5 = (bf16[48,1536]{1,0:T(8,128)(2,1)S(1)}, bf16[48,1536]{1,0:T(8,128)(2,1)S(1)}, u32[]{:S(2)}, u32[]{:S(2)}) collective-permute-start(bf16[48,1536]{1,0:T(8,128)(2,1)S(1)} %get-tuple-element.83), channel_id=1, source_target_pairs={{0,2},{1,3},{2,0},{3,1},{4,6},{5,7},{6,4},{7,5},{8,10},{9,11},{10,... | collective-permute-start | bytes 442376 | tf_op jit(solution)/shard_map/ppermute | solution.py:605
  20.0 1.7 %collective-permute-start.4 = (bf16[48,1536]{1,0:T(8,128)(2,1)S(1)}, bf16[48,1536]{1,0:T(8,128)(2,1)S(1)}, u32[]{:S(2)}, u32[]{:S(2)}) collective-permute-start(bf16[48,1536]{1,0:T(8,128)(2,1)S(1)} %get-tuple-element.84), channel_id=1, source_target_pairs={{0,4},{1,5},{2,6},{3,7},{4,0},{5,1},{6,2},{7,3},{8,12},{9,13},{10,... | collective-permute-start | bytes 442376 | tf_op jit(solution)/shard_map/ppermute | solution.py:605
  21.8 0.5 %shard_map.195.refs_7_.refs_1_ = bf16[64,768]{1,0:T(8,128)(2,1)S(1)} custom-call(bf16[256,384]{1,0:T(8,128)(2,1)S(1)} %get-tuple-element.67.refs_0_, bf16[1536,768]{1,0:T(8,128)(2,1)S(1)} %get-tuple-element.49.refs_9_.refs_1_), custom_call_target="tpu_custom_call" | custom-call | tf_op jit(solution)/shard_map/pallas_call | solution.py:568
  22.3 0.8 %shard_map.196 = (bf16[96,384]{1,0:T(8,128)(2,1)S(1)}, bf16[256,384]{1,0:T(8,128)(2,1)S(1)}) custom-call(bf16[256,1152]{1,0:T(8,128)(2,1)S(1)} %get-tuple-element.61.refs_0_, bf16[384,1152]{1,0:T(8,128)(2,1)S(1)} %get-tuple-element.42.refs_2_.refs_1_, f32[256,384]{1,0:T(8,128)S(1)} %get-tuple-element.62.refs_2_, f32[256,1]{1,0:T(8,128)S(1)} %get-tuple-element.63.refs_3_, ...), custom_call_target="tpu_custom_call" | custom-call | tf_op jit(solution)/shard_map/pallas_call | solution.py:568
  23.1 2.1 %collective-permute-start.1 = (bf16[96,384]{1,0:T(8,128)(2,1)S(1)}, bf16[96,384]{1,0:T(8,128)(2,1)S(1)}, u32[]{:S(2)}, u32[]{:S(2)}) collective-permute-start(bf16[96,384]{1,0:T(8,128)(2,1)S(1)} %get-tuple-element.69), channel_id=1, source_target_pairs={{4,0},{8,4},{12,8},{16,12},{20,16},{24,20},{28,24},{0,28},{5,1},{9... | collective-permute-start | bytes 221192 | tf_op jit(solution)/shard_map/ppermute | solution.py:689
  25.2 0.8 %collective-permute-done.3 = bf16[48,1536]{1,0:T(8,128)(2,1)S(1)} collective-permute-done((bf16[48,1536]{1,0:T(8,128)(2,1)S(1)}, bf16[48,1536]{1,0:T(8,128)(2,1)S(1)}, u32[]{:S(2)}, u32[]{:S(2)}) %collective-permute-start.3) | collective-permute-done | bytes 147488 | tf_op jit(solution)/shard_map/ppermute | solution.py:605
  25.9 1.7 %collective-permute-done.5 = bf16[48,1536]{1,0:T(8,128)(2,1)S(1)} collective-permute-done((bf16[48,1536]{1,0:T(8,128)(2,1)S(1)}, bf16[48,1536]{1,0:T(8,128)(2,1)S(1)}, u32[]{:S(2)}, u32[]{:S(2)}) %collective-permute-start.5) | collective-permute-done | bytes 147488 | tf_op jit(solution)/shard_map/ppermute | solution.py:605
  27.7 1.6 %collective-permute-done.4 = bf16[48,1536]{1,0:T(8,128)(2,1)S(1)} collective-permute-done((bf16[48,1536]{1,0:T(8,128)(2,1)S(1)}, bf16[48,1536]{1,0:T(8,128)(2,1)S(1)}, u32[]{:S(2)}, u32[]{:S(2)}) %collective-permute-start.4) | collective-permute-done | bytes 147488 | tf_op jit(solution)/shard_map/ppermute | solution.py:605
  29.3 0.1 fusion.2
  29.4 0.1 collective-permute-start.8
  29.5 2.4 %collective-permute-start.7 = (bf16[12,1536]{1,0:T(8,128)(2,1)S(1)}, bf16[12,1536]{1,0:T(8,128)(2,1)S(1)}, u32[]{:S(2)}, u32[]{:S(2)}) collective-permute-start(bf16[12,1536]{1,0:T(8,128)(2,1)S(1)} %get-tuple-element.86), channel_id=1, source_target_pairs={{0,16},{1,17},{2,18},{3,19},{4,20},{5,21},{6,22},{7,23},{8,24},{9,... | collective-permute-start | bytes 110600 | tf_op jit(solution)/shard_map/ppermute | solution.py:605
  31.8 2.0 %collective-permute-start.6 = (bf16[12,1536]{1,0:T(8,128)(2,1)S(1)}, bf16[12,1536]{1,0:T(8,128)(2,1)S(1)}, u32[]{:S(2)}, u32[]{:S(2)}) collective-permute-start(bf16[12,1536]{1,0:T(8,128)(2,1)S(1)} %get-tuple-element.87), channel_id=1, source_target_pairs={{0,24},{1,25},{2,26},{3,27},{4,28},{5,29},{6,30},{7,31},{8,16},{9,... | collective-permute-start | bytes 110600 | tf_op jit(solution)/shard_map/ppermute | solution.py:605
  33.9 0.0 collective-permute-done.1.refs_2_
  33.9 1.0 %shard_map.197 = (bf16[14,14,384]{2,1,0:T(8,128)(2,1)}, bf16[7,7,768]{2,1,0:T(8,128)(2,1)}) custom-call(bf16[256,384]{1,0:T(8,128)(2,1)S(1)} %get-tuple-element.68.refs_0_, bf16[64,768]{1,0:T(8,128)(2,1)S(1)} %shard_map.195.refs_7_.refs_1_, bf16[96,384]{1,0:T(8,128)(2,1)S(1)} %collective-permute-done.1.refs_2_, ...), custom_call_target="tpu_custom_call" | custom-call | tf_op jit(solution)/shard_map/pallas_call | solution.py:568
  34.8 0.0 collective-permute-done.8.refs_3_
  34.9 0.0 collective-permute-done.7.refs_2_
  34.9 2.9 %collective-permute-done.6.refs_1_ = bf16[12,1536]{1,0:T(8,128)(2,1)S(1)} collective-permute-done((bf16[12,1536]{1,0:T(8,128)(2,1)S(1)}, bf16[12,1536]{1,0:T(8,128)(2,1)S(1)}, u32[]{:S(2)}, u32[]{:S(2)}) %collective-permute-start.6) | collective-permute-done | bytes 36896 | tf_op jit(solution)/shard_map/ppermute | solution.py:605
  37.7 0.7 %shard_map.198 = (f32[108,128]{1,0:T(8,128)}, f32[36,128]{1,0:T(8,128)}) custom-call(f32[48,1536]{1,0:T(8,128)S(1)} %get-tuple-element.79.refs_0_, bf16[12,1536]{1,0:T(8,128)(2,1)S(1)} %collective-permute-done.6.refs_1_, bf16[12,1536]{1,0:T(8,128)(2,1)S(1)} %collective-permute-done.7.refs_2_, bf16[12,1536]{1,0:T(8,128)(2,1)S(1)} %collective-permute-done.8.refs_3_), custom_call_target="tpu_custom_call" | custom-call | tf_op jit(solution)/shard_map/pallas_call | solution.py:568
  (2 shorter events, 0.1 us)
Async XLA Ops:
  2.0 8.4 %collective-permute-start = (bf16[96,384]{1,0:T(8,128)(2,1)S(1)}, bf16[96,384]{1,0:T(8,128)(2,1)S(1)}, u32[]{:S(2)}, u32[]{:S(2)}) collective-permute-start(bf16[96,384]{1,0:T(8,128)(2,1)S(1)} %shard_map.192), channel_id=1, source_target_pairs={{28,0},{0,4},{4,8},{8,12},{12,16},{16,20},{20,24},{24,28},{29,1},{... | collective-permute-start | bytes 221192 | tf_op jit(solution)/shard_map/ppermute | solution.py:689
  15.9 2.1 %collective-permute-start.2 = (bf16[192,1536]{1,0:T(8,128)(2,1)S(1)}, bf16[192,1536]{1,0:T(8,128)(2,1)S(1)}, u32[]{:S(2)}, u32[]{:S(2)}) collective-permute-start(bf16[192,1536]{1,0:T(8,128)(2,1)S(1)} %get-tuple-element.75), channel_id=1, source_target_pairs={{0,1},{1,0},{2,3},{3,2},{4,5},{5,4},{6,7},{7,6},{8,9},{9,8},{10,11... | collective-permute-start | bytes 1769480 | tf_op jit(solution)/shard_map/ppermute | solution.py:605
  18.2 7.7 %collective-permute-start.3 = (bf16[48,1536]{1,0:T(8,128)(2,1)S(1)}, bf16[48,1536]{1,0:T(8,128)(2,1)S(1)}, u32[]{:S(2)}, u32[]{:S(2)}) collective-permute-start(bf16[48,1536]{1,0:T(8,128)(2,1)S(1)} %get-tuple-element.82), channel_id=1, source_target_pairs={{0,6},{1,7},{2,4},{3,5},{4,2},{5,3},{6,0},{7,1},{8,14},{9,15},{10,... | collective-permute-start | bytes 442376 | tf_op jit(solution)/shard_map/ppermute | solution.py:605
  18.9 8.8 %collective-permute-start.5 = (bf16[48,1536]{1,0:T(8,128)(2,1)S(1)}, bf16[48,1536]{1,0:T(8,128)(2,1)S(1)}, u32[]{:S(2)}, u32[]{:S(2)}) collective-permute-start(bf16[48,1536]{1,0:T(8,128)(2,1)S(1)} %get-tuple-element.83), channel_id=1, source_target_pairs={{0,2},{1,3},{2,0},{3,1},{4,6},{5,7},{6,4},{7,5},{8,10},{9,11},{10,... | collective-permute-start | bytes 442376 | tf_op jit(solution)/shard_map/ppermute | solution.py:605
  20.0 9.2 %collective-permute-start.4 = (bf16[48,1536]{1,0:T(8,128)(2,1)S(1)}, bf16[48,1536]{1,0:T(8,128)(2,1)S(1)}, u32[]{:S(2)}, u32[]{:S(2)}) collective-permute-start(bf16[48,1536]{1,0:T(8,128)(2,1)S(1)} %get-tuple-element.84), channel_id=1, source_target_pairs={{0,4},{1,5},{2,6},{3,7},{4,0},{5,1},{6,2},{7,3},{8,12},{9,13},{10,... | collective-permute-start | bytes 442376 | tf_op jit(solution)/shard_map/ppermute | solution.py:605
  23.1 10.8 %collective-permute-start.1 = (bf16[96,384]{1,0:T(8,128)(2,1)S(1)}, bf16[96,384]{1,0:T(8,128)(2,1)S(1)}, u32[]{:S(2)}, u32[]{:S(2)}) collective-permute-start(bf16[96,384]{1,0:T(8,128)(2,1)S(1)} %get-tuple-element.69), channel_id=1, source_target_pairs={{4,0},{8,4},{12,8},{16,12},{20,16},{24,20},{28,24},{0,28},{5,1},{9... | collective-permute-start | bytes 221192 | tf_op jit(solution)/shard_map/ppermute | solution.py:689
  29.4 5.4 %collective-permute-start.8 = (bf16[12,1536]{1,0:T(8,128)(2,1)S(1)}, bf16[12,1536]{1,0:T(8,128)(2,1)S(1)}, u32[]{:S(2)}, u32[]{:S(2)}) collective-permute-start(bf16[12,1536]{1,0:T(8,128)(2,1)S(1)} %get-tuple-element.85), channel_id=1, source_target_pairs={{0,8},{1,9},{2,10},{3,11},{4,12},{5,13},{6,14},{7,15},{8,0},{9,1},... | collective-permute-start | bytes 110600 | tf_op jit(solution)/shard_map/ppermute | solution.py:605
  29.5 5.4 %collective-permute-start.7 = (bf16[12,1536]{1,0:T(8,128)(2,1)S(1)}, bf16[12,1536]{1,0:T(8,128)(2,1)S(1)}, u32[]{:S(2)}, u32[]{:S(2)}) collective-permute-start(bf16[12,1536]{1,0:T(8,128)(2,1)S(1)} %get-tuple-element.86), channel_id=1, source_target_pairs={{0,16},{1,17},{2,18},{3,19},{4,20},{5,21},{6,22},{7,23},{8,24},{9,... | collective-permute-start | bytes 110600 | tf_op jit(solution)/shard_map/ppermute | solution.py:605
  31.8 5.9 %collective-permute-start.6 = (bf16[12,1536]{1,0:T(8,128)(2,1)S(1)}, bf16[12,1536]{1,0:T(8,128)(2,1)S(1)}, u32[]{:S(2)}, u32[]{:S(2)}) collective-permute-start(bf16[12,1536]{1,0:T(8,128)(2,1)S(1)} %get-tuple-element.87), channel_id=1, source_target_pairs={{0,24},{1,25},{2,26},{3,27},{4,28},{5,29},{6,30},{7,31},{8,16},{9,... | collective-permute-start | bytes 110600 | tf_op jit(solution)/shard_map/ppermute | solution.py:605
where the time goes:
time: 38.5 us; the launch traced here: 38.4 us
  Pallas kernels  13.3 us (35%)
  starting transfers between devices  13.2 us (34%)
  waiting for transfers between devices  10.9 us (28%)
  between operations  0.74 us (2%)
    pallas_call x7, Pallas kernels, call(): pl.pallas_call(body, out_shape=[space(m)(getattr(m, 'array', m).shape, ge...  13.3 us
    ppermute x7, waiting for transfers between devices, exchange(): lax.ppermute(block, ('azim', 'frame'), [(i, i ^ mask) for i in range(memb...  8.98 us
    ppermute x7, starting transfers between devices, exchange(): lax.ppermute(block, ('azim', 'frame'), [(i, i ^ mask) for i in range(memb...  8.07 us
    ppermute x2, starting transfers between devices, from_behind(): lax.ppermute(block, axis, [((i - distance) % size, i) for i in range(size)])  5.09 us
    ppermute x2, waiting for transfers between devices, from_behind(): lax.ppermute(block, axis, [((i - distance) % size, i) for i in range(size)])  1.89 us
  transfers between devices with their start and end apart: 9, of which 6 were waited for; matrix products, arithmetic and copies ran while one was open for 0% of the time, Pallas kernels for 15%

commit v1 on v0

--- a/solution.py
+++ b/solution.py
@@ -640,11 +640,11 @@
     return total[: widths[0]], total[widths[0] :]
 
 
-def swap(total, weights):
+def swap(total, weights, blocks):
     count = 1 << len(weights)
     rows = total.shape[0] // count
     gots = []
-    for block in range(count - 1, 0, -1):
+    for block in blocks:
         mask = sum(w for i, w in enumerate(weights) if block >> (len(weights) - 1 - i) & 1)
         part = total[block * rows : (block + 1) * rows].astype(jnp.bfloat16)
         gots.append(exchange(part, mask))
@@ -672,9 +672,9 @@
         whole = jnp.concatenate([kept, sent.astype(jnp.float32)], 0)
         return scatter_flat((whole[:, :split], whole[:, split:]))
     total = kept + exchange(sent, groups[0][0]).astype(jnp.float32)
-    gots = swap(total, groups[1])
+    gots = swap(total, groups[1], (3, 2, 1))
     total = sum((got.astype(jnp.float32) for got in gots), total[: gots[0].shape[0]])
-    gots = swap(total, groups[2])
+    gots = swap(total, groups[2], (2, 1, 3))
     rows = gots[0].shape[0]
     attend_grad, output_grad = call(
         functools.partial(finish_kernel, split),

time: 38.5 us -> 37.2 us (0.966)
  waiting for transfers between devices: 10.9 us -> 9.58 us
    ppermute x7, waiting for transfers between devices: 8.98 us -> 7.68 us  [exchange(): lax.ppermute(block, ('azim', 'frame'), [(i, i ^ mask) for i in range(memb...]
  transfers between devices with their start and end apart: 9 -> 9, of which waited for: 6 -> 7; matrix products, arithmetic and copies ran while one was open for 0% -> 0% of each run, Pallas kernels for 15% -> 16%
where the time goes in v1:
time: 37.2 us; the launch traced here: 37.1 us
  Pallas kernels  13.3 us (36%)
  starting transfers between devices  13.2 us (35%)
  waiting for transfers between devices  9.58 us (26%)
  between operations  0.72 us (2%)
    pallas_call x7, Pallas kernels, call(): pl.pallas_call(body, out_shape=[space(m)(getattr(m, 'array', m).shape, ge...  13.3 us
    ppermute x7, starting transfers between devices, exchange(): lax.ppermute(block, ('azim', 'frame'), [(i, i ^ mask) for i in range(memb...  8.08 us
    ppermute x7, waiting for transfers between devices, exchange(): lax.ppermute(block, ('azim', 'frame'), [(i, i ^ mask) for i in range(memb...  7.68 us
    ppermute x2, starting transfers between devices, from_behind(): lax.ppermute(block, axis, [((i - distance) % size, i) for i in range(size)])  5.09 us
    ppermute x2, waiting for transfers between devices, from_behind(): lax.ppermute(block, axis, [((i - distance) % size, i) for i in range(size)])  1.89 us
  transfers between devices with their start and end apart: 9, of which 7 were waited for; matrix products, arithmetic and copies ran while one was open for 0% of the time, Pallas kernels for 16%

profile of v1, /device:TPU:0, one launch (start us, length us, event | category | flops | bytes accessed | tf_op | source)
XLA Modules:
  0.0 37.1 jit_solution(11632811110976243645)
XLA Ops:
  0.6 1.3 %shard_map.192 = bf16[96,384]{1,0:T(8,128)(2,1)S(1)} custom-call(bf16[14,14,384]{2,1,0:T(8,128)(2,1)} %bitcast.7, bf16[7,7,768]{2,1,0:T(8,128)(2,1)} %bitcast.9, bf16[64,224]{1,0:T(8,128)(2,1)} %constant.21.clone.refs_2_, bf16[16,112]{1,0:T(8,128)(2,1)} %constant.22.clone.refs_3_), custom_call_target="tpu_custom_call" | custom-call | tf_op jit(solution)/shard_map/pallas_call | solution.py:568
  2.0 3.0 %collective-permute-start = (bf16[96,384]{1,0:T(8,128)(2,1)S(1)}, bf16[96,384]{1,0:T(8,128)(2,1)S(1)}, u32[]{:S(2)}, u32[]{:S(2)}) collective-permute-start(bf16[96,384]{1,0:T(8,128)(2,1)S(1)} %shard_map.192), channel_id=1, source_target_pairs={{28,0},{0,4},{4,8},{8,12},{12,16},{16,20},{20,24},{24,28},{29,1},{... | collective-permute-start | bytes 221192 | tf_op jit(solution)/shard_map/ppermute | solution.py:689
  5.0 3.5 %shard_map.193 = (bf16[256,288]{1,0:T(8,128)(2,1)S(1)}, bf16[384,1152]{1,0:T(8,128)(2,1)S(1)}, bf16[256,128]{1,0:T(8,128)(2,1)S(1)}, bf16[1536,768]{1,0:T(8,128)...) custom-call(bf16[14,14,384]{2,1,0:T(8,128)(2,1)} %bitcast.8, ...), custom_call_target="tpu_custom_call" | custom-call | tf_op jit(solution)/shard_map/pallas_call | solution.py:568
  8.5 1.9 %collective-permute-done.refs_0_ = bf16[96,384]{1,0:T(8,128)(2,1)S(1)} collective-permute-done((bf16[96,384]{1,0:T(8,128)(2,1)S(1)}, bf16[96,384]{1,0:T(8,128)(2,1)S(1)}, u32[]{:S(2)}, u32[]{:S(2)}) %collective-permute-start) | collective-permute-done | bytes 73760 | tf_op jit(solution)/shard_map/ppermute | solution.py:689
  10.4 5.5 %shard_map.194 = (f32[192,1536]{1,0:T(8,128)S(1)}, bf16[192,1536]{1,0:T(8,128)(2,1)S(1)}, bf16[256,1152]{1,0:T(8,128)(2,1)S(1)}, f32[256,384]{1,0:T(8,128)S(1)},...) custom-call(bf16[96,384]{1,0:T(8,128)(2,1)S(1)} %collective-permute-done.refs_0_, ...), custom_call_target="tpu_custom_call" | custom-call | tf_op jit(solution)/shard_map/pallas_call | solution.py:568
  15.9 0.1 collective-permute-start.2
  16.0 2.0 %collective-permute-done.2 = bf16[192,1536]{1,0:T(8,128)(2,1)S(1)} collective-permute-done((bf16[192,1536]{1,0:T(8,128)(2,1)S(1)}, bf16[192,1536]{1,0:T(8,128)(2,1)S(1)}, u32[]{:S(2)}, u32[]{:S(2)}) %collective-permute-start.2) | collective-permute-done | bytes 589856 | tf_op jit(solution)/shard_map/ppermute | solution.py:605
  18.0 0.2 fusion.4
  18.2 0.7 %collective-permute-start.3 = (bf16[48,1536]{1,0:T(8,128)(2,1)S(1)}, bf16[48,1536]{1,0:T(8,128)(2,1)S(1)}, u32[]{:S(2)}, u32[]{:S(2)}) collective-permute-start(bf16[48,1536]{1,0:T(8,128)(2,1)S(1)} %get-tuple-element.82), channel_id=1, source_target_pairs={{0,6},{1,7},{2,4},{3,5},{4,2},{5,3},{6,0},{7,1},{8,14},{9,15},{10,... | collective-permute-start | bytes 442376 | tf_op jit(solution)/shard_map/ppermute | solution.py:605
  18.9 1.1 %collective-permute-start.5 = (bf16[48,1536]{1,0:T(8,128)(2,1)S(1)}, bf16[48,1536]{1,0:T(8,128)(2,1)S(1)}, u32[]{:S(2)}, u32[]{:S(2)}) collective-permute-start(bf16[48,1536]{1,0:T(8,128)(2,1)S(1)} %get-tuple-element.83), channel_id=1, source_target_pairs={{0,2},{1,3},{2,0},{3,1},{4,6},{5,7},{6,4},{7,5},{8,10},{9,11},{10,... | collective-permute-start | bytes 442376 | tf_op jit(solution)/shard_map/ppermute | solution.py:605
  20.0 1.7 %collective-permute-start.4 = (bf16[48,1536]{1,0:T(8,128)(2,1)S(1)}, bf16[48,1536]{1,0:T(8,128)(2,1)S(1)}, u32[]{:S(2)}, u32[]{:S(2)}) collective-permute-start(bf16[48,1536]{1,0:T(8,128)(2,1)S(1)} %get-tuple-element.84), channel_id=1, source_target_pairs={{0,4},{1,5},{2,6},{3,7},{4,0},{5,1},{6,2},{7,3},{8,12},{9,13},{10,... | collective-permute-start | bytes 442376 | tf_op jit(solution)/shard_map/ppermute | solution.py:605
  21.8 0.5 %shard_map.195.refs_7_.refs_1_ = bf16[64,768]{1,0:T(8,128)(2,1)S(1)} custom-call(bf16[256,384]{1,0:T(8,128)(2,1)S(1)} %get-tuple-element.67.refs_0_, bf16[1536,768]{1,0:T(8,128)(2,1)S(1)} %get-tuple-element.49.refs_9_.refs_1_), custom_call_target="tpu_custom_call" | custom-call | tf_op jit(solution)/shard_map/pallas_call | solution.py:568
  22.3 0.8 %shard_map.196 = (bf16[96,384]{1,0:T(8,128)(2,1)S(1)}, bf16[256,384]{1,0:T(8,128)(2,1)S(1)}) custom-call(bf16[256,1152]{1,0:T(8,128)(2,1)S(1)} %get-tuple-element.61.refs_0_, bf16[384,1152]{1,0:T(8,128)(2,1)S(1)} %get-tuple-element.42.refs_2_.refs_1_, f32[256,384]{1,0:T(8,128)S(1)} %get-tuple-element.62.refs_2_, f32[256,1]{1,0:T(8,128)S(1)} %get-tuple-element.63.refs_3_, ...), custom_call_target="tpu_custom_call" | custom-call | tf_op jit(solution)/shard_map/pallas_call | solution.py:568
  23.1 2.1 %collective-permute-start.1 = (bf16[96,384]{1,0:T(8,128)(2,1)S(1)}, bf16[96,384]{1,0:T(8,128)(2,1)S(1)}, u32[]{:S(2)}, u32[]{:S(2)}) collective-permute-start(bf16[96,384]{1,0:T(8,128)(2,1)S(1)} %get-tuple-element.69), channel_id=1, source_target_pairs={{4,0},{8,4},{12,8},{16,12},{20,16},{24,20},{28,24},{0,28},{5,1},{9... | collective-permute-start | bytes 221192 | tf_op jit(solution)/shard_map/ppermute | solution.py:689
  25.2 0.8 %collective-permute-done.3 = bf16[48,1536]{1,0:T(8,128)(2,1)S(1)} collective-permute-done((bf16[48,1536]{1,0:T(8,128)(2,1)S(1)}, bf16[48,1536]{1,0:T(8,128)(2,1)S(1)}, u32[]{:S(2)}, u32[]{:S(2)}) %collective-permute-start.3) | collective-permute-done | bytes 147488 | tf_op jit(solution)/shard_map/ppermute | solution.py:605
  25.9 1.7 %collective-permute-done.5 = bf16[48,1536]{1,0:T(8,128)(2,1)S(1)} collective-permute-done((bf16[48,1536]{1,0:T(8,128)(2,1)S(1)}, bf16[48,1536]{1,0:T(8,128)(2,1)S(1)}, u32[]{:S(2)}, u32[]{:S(2)}) %collective-permute-start.5) | collective-permute-done | bytes 147488 | tf_op jit(solution)/shard_map/ppermute | solution.py:605
  27.7 1.6 %collective-permute-done.4 = bf16[48,1536]{1,0:T(8,128)(2,1)S(1)} collective-permute-done((bf16[48,1536]{1,0:T(8,128)(2,1)S(1)}, bf16[48,1536]{1,0:T(8,128)(2,1)S(1)}, u32[]{:S(2)}, u32[]{:S(2)}) %collective-permute-start.4) | collective-permute-done | bytes 147488 | tf_op jit(solution)/shard_map/ppermute | solution.py:605
  29.3 0.1 fusion.2
  29.4 1.9 %collective-permute-start.8 = (bf16[12,1536]{1,0:T(8,128)(2,1)S(1)}, bf16[12,1536]{1,0:T(8,128)(2,1)S(1)}, u32[]{:S(2)}, u32[]{:S(2)}) collective-permute-start(bf16[12,1536]{1,0:T(8,128)(2,1)S(1)} %get-tuple-element.85), channel_id=1, source_target_pairs={{0,24},{1,25},{2,26},{3,27},{4,28},{5,29},{6,30},{7,31},{8,16},{9,... | collective-permute-start | bytes 110600 | tf_op jit(solution)/shard_map/ppermute | solution.py:605
  31.3 0.0 collective-permute-start.7
  31.3 2.6 %collective-permute-start.6 = (bf16[12,1536]{1,0:T(8,128)(2,1)S(1)}, bf16[12,1536]{1,0:T(8,128)(2,1)S(1)}, u32[]{:S(2)}, u32[]{:S(2)}) collective-permute-start(bf16[12,1536]{1,0:T(8,128)(2,1)S(1)} %get-tuple-element.87), channel_id=1, source_target_pairs={{0,16},{1,17},{2,18},{3,19},{4,20},{5,21},{6,22},{7,23},{8,24},{9,... | collective-permute-start | bytes 110600 | tf_op jit(solution)/shard_map/ppermute | solution.py:605
  33.9 0.0 collective-permute-done.1.refs_2_
  33.9 1.0 %shard_map.197 = (bf16[14,14,384]{2,1,0:T(8,128)(2,1)}, bf16[7,7,768]{2,1,0:T(8,128)(2,1)}) custom-call(bf16[256,384]{1,0:T(8,128)(2,1)S(1)} %get-tuple-element.68.refs_0_, bf16[64,768]{1,0:T(8,128)(2,1)S(1)} %shard_map.195.refs_7_.refs_1_, bf16[96,384]{1,0:T(8,128)(2,1)S(1)} %collective-permute-done.1.refs_2_, ...), custom_call_target="tpu_custom_call" | custom-call | tf_op jit(solution)/shard_map/pallas_call | solution.py:568
  34.8 1.1 %collective-permute-done.8.refs_3_ = bf16[12,1536]{1,0:T(8,128)(2,1)S(1)} collective-permute-done((bf16[12,1536]{1,0:T(8,128)(2,1)S(1)}, bf16[12,1536]{1,0:T(8,128)(2,1)S(1)}, u32[]{:S(2)}, u32[]{:S(2)}) %collective-permute-start.8) | collective-permute-done | bytes 36896 | tf_op jit(solution)/shard_map/ppermute | solution.py:605
  35.9 0.0 collective-permute-done.7.refs_2_
  35.9 0.5 %collective-permute-done.6.refs_1_ = bf16[12,1536]{1,0:T(8,128)(2,1)S(1)} collective-permute-done((bf16[12,1536]{1,0:T(8,128)(2,1)S(1)}, bf16[12,1536]{1,0:T(8,128)(2,1)S(1)}, u32[]{:S(2)}, u32[]{:S(2)}) %collective-permute-start.6) | collective-permute-done | bytes 36896 | tf_op jit(solution)/shard_map/ppermute | solution.py:605
  36.4 0.7 %shard_map.198 = (f32[108,128]{1,0:T(8,128)}, f32[36,128]{1,0:T(8,128)}) custom-call(f32[48,1536]{1,0:T(8,128)S(1)} %get-tuple-element.79.refs_0_, bf16[12,1536]{1,0:T(8,128)(2,1)S(1)} %collective-permute-done.6.refs_1_, bf16[12,1536]{1,0:T(8,128)(2,1)S(1)} %collective-permute-done.7.refs_2_, bf16[12,1536]{1,0:T(8,128)(2,1)S(1)} %collective-permute-done.8.refs_3_), custom_call_target="tpu_custom_call" | custom-call | tf_op jit(solution)/shard_map/pallas_call | solution.py:568
  (2 shorter events, 0.1 us)
Async XLA Ops:
  2.0 8.4 %collective-permute-start = (bf16[96,384]{1,0:T(8,128)(2,1)S(1)}, bf16[96,384]{1,0:T(8,128)(2,1)S(1)}, u32[]{:S(2)}, u32[]{:S(2)}) collective-permute-start(bf16[96,384]{1,0:T(8,128)(2,1)S(1)} %shard_map.192), channel_id=1, source_target_pairs={{28,0},{0,4},{4,8},{8,12},{12,16},{16,20},{20,24},{24,28},{29,1},{... | collective-permute-start | bytes 221192 | tf_op jit(solution)/shard_map/ppermute | solution.py:689
  15.9 2.1 %collective-permute-start.2 = (bf16[192,1536]{1,0:T(8,128)(2,1)S(1)}, bf16[192,1536]{1,0:T(8,128)(2,1)S(1)}, u32[]{:S(2)}, u32[]{:S(2)}) collective-permute-start(bf16[192,1536]{1,0:T(8,128)(2,1)S(1)} %get-tuple-element.75), channel_id=1, source_target_pairs={{0,1},{1,0},{2,3},{3,2},{4,5},{5,4},{6,7},{7,6},{8,9},{9,8},{10,11... | collective-permute-start | bytes 1769480 | tf_op jit(solution)/shard_map/ppermute | solution.py:605
  18.2 7.7 %collective-permute-start.3 = (bf16[48,1536]{1,0:T(8,128)(2,1)S(1)}, bf16[48,1536]{1,0:T(8,128)(2,1)S(1)}, u32[]{:S(2)}, u32[]{:S(2)}) collective-permute-start(bf16[48,1536]{1,0:T(8,128)(2,1)S(1)} %get-tuple-element.82), channel_id=1, source_target_pairs={{0,6},{1,7},{2,4},{3,5},{4,2},{5,3},{6,0},{7,1},{8,14},{9,15},{10,... | collective-permute-start | bytes 442376 | tf_op jit(solution)/shard_map/ppermute | solution.py:605
  18.9 8.8 %collective-permute-start.5 = (bf16[48,1536]{1,0:T(8,128)(2,1)S(1)}, bf16[48,1536]{1,0:T(8,128)(2,1)S(1)}, u32[]{:S(2)}, u32[]{:S(2)}) collective-permute-start(bf16[48,1536]{1,0:T(8,128)(2,1)S(1)} %get-tuple-element.83), channel_id=1, source_target_pairs={{0,2},{1,3},{2,0},{3,1},{4,6},{5,7},{6,4},{7,5},{8,10},{9,11},{10,... | collective-permute-start | bytes 442376 | tf_op jit(solution)/shard_map/ppermute | solution.py:605
  20.0 9.2 %collective-permute-start.4 = (bf16[48,1536]{1,0:T(8,128)(2,1)S(1)}, bf16[48,1536]{1,0:T(8,128)(2,1)S(1)}, u32[]{:S(2)}, u32[]{:S(2)}) collective-permute-start(bf16[48,1536]{1,0:T(8,128)(2,1)S(1)} %get-tuple-element.84), channel_id=1, source_target_pairs={{0,4},{1,5},{2,6},{3,7},{4,0},{5,1},{6,2},{7,3},{8,12},{9,13},{10,... | collective-permute-start | bytes 442376 | tf_op jit(solution)/shard_map/ppermute | solution.py:605
  23.1 10.8 %collective-permute-start.1 = (bf16[96,384]{1,0:T(8,128)(2,1)S(1)}, bf16[96,384]{1,0:T(8,128)(2,1)S(1)}, u32[]{:S(2)}, u32[]{:S(2)}) collective-permute-start(bf16[96,384]{1,0:T(8,128)(2,1)S(1)} %get-tuple-element.69), channel_id=1, source_target_pairs={{4,0},{8,4},{12,8},{16,12},{20,16},{24,20},{28,24},{0,28},{5,1},{9... | collective-permute-start | bytes 221192 | tf_op jit(solution)/shard_map/ppermute | solution.py:689
  29.4 6.5 %collective-permute-start.8 = (bf16[12,1536]{1,0:T(8,128)(2,1)S(1)}, bf16[12,1536]{1,0:T(8,128)(2,1)S(1)}, u32[]{:S(2)}, u32[]{:S(2)}) collective-permute-start(bf16[12,1536]{1,0:T(8,128)(2,1)S(1)} %get-tuple-element.85), channel_id=1, source_target_pairs={{0,24},{1,25},{2,26},{3,27},{4,28},{5,29},{6,30},{7,31},{8,16},{9,... | collective-permute-start | bytes 110600 | tf_op jit(solution)/shard_map/ppermute | solution.py:605
  31.3 4.6 %collective-permute-start.7 = (bf16[12,1536]{1,0:T(8,128)(2,1)S(1)}, bf16[12,1536]{1,0:T(8,128)(2,1)S(1)}, u32[]{:S(2)}, u32[]{:S(2)}) collective-permute-start(bf16[12,1536]{1,0:T(8,128)(2,1)S(1)} %get-tuple-element.86), channel_id=1, source_target_pairs={{0,8},{1,9},{2,10},{3,11},{4,12},{5,13},{6,14},{7,15},{8,0},{9,1},... | collective-permute-start | bytes 110600 | tf_op jit(solution)/shard_map/ppermute | solution.py:605
  31.3 5.1 %collective-permute-start.6 = (bf16[12,1536]{1,0:T(8,128)(2,1)S(1)}, bf16[12,1536]{1,0:T(8,128)(2,1)S(1)}, u32[]{:S(2)}, u32[]{:S(2)}) collective-permute-start(bf16[12,1536]{1,0:T(8,128)(2,1)S(1)} %get-tuple-element.87), channel_id=1, source_target_pairs={{0,16},{1,17},{2,18},{3,19},{4,20},{5,21},{6,22},{7,23},{8,24},{9,... | collective-permute-start | bytes 110600 | tf_op jit(solution)/shard_map/ppermute | solution.py:605

commit v2 on v1

--- a/solution.py
+++ b/solution.py
@@ -43,7 +43,7 @@
         self.window_rows, self.local_rows = self.windows * SLOT, self.local_windows * SLOT
         self.stride = up(cols, 16)
         self.own_rows = rows * self.stride
-        self.west_rows = up(rows * self.west, 16)
+        self.west_rows = up(rows * self.west, 8)
         self.quad_lines, self.quad_cols, self.quad_west = rows // 2, cols // 2, self.west // 2
         self.quad_stride = up(self.quad_cols, 8)
         self.quad_count = up(self.quad_lines * self.quad_stride, 16)
@@ -309,7 +309,7 @@
     states = [()] * len(jobs)
     fillers = list(fillers)
     for turn in range(len(jobs) + len(stages) - 1):
-        for depth, stage in reversed(list(enumerate(stages))):
+        for depth, stage in enumerate(stages):
             at = turn - depth
             if 0 <= at < len(jobs):
                 states[at] = stage(jobs[at], *states[at])
@@ -640,15 +640,18 @@
     return total[: widths[0]], total[widths[0] :]
 
 
-def swap(total, weights, blocks):
-    count = 1 << len(weights)
-    rows = total.shape[0] // count
-    gots = []
-    for block in blocks:
-        mask = sum(w for i, w in enumerate(weights) if block >> (len(weights) - 1 - i) & 1)
-        part = total[block * rows : (block + 1) * rows].astype(jnp.bfloat16)
-        gots.append(exchange(part, mask))
-    return gots
+def send_block(part, weights, block):
+    mask = sum(w for i, w in enumerate(weights) if block >> (len(weights) - 1 - i) & 1)
+    return exchange(part.astype(jnp.bfloat16), mask)
+
+
+def add_kernel(first, kept, got, *totals):
+    at = 0
+    for total in totals:
+        rows = total.ref.shape[0]
+        own = kept.ref[first + at : first + at + rows, :]
+        total.ref[...] = (own + got.ref[at : at + rows, :].astype(jnp.float32)).astype(total.ref.dtype)
+        at += rows
 
 
 def finish_kernel(split, total, *rest):
@@ -671,11 +674,19 @@
     if channels % (1 << len(sum(groups, []))):
         whole = jnp.concatenate([kept, sent.astype(jnp.float32)], 0)
         return scatter_flat((whole[:, :split], whole[:, split:]))
-    total = kept + exchange(sent, groups[0][0]).astype(jnp.float32)
-    gots = swap(total, groups[1], (3, 2, 1))
-    total = sum((got.astype(jnp.float32) for got in gots), total[: gots[0].shape[0]])
-    gots = swap(total, groups[2], (2, 1, 3))
-    rows = gots[0].shape[0]
+    count = 1 << len(groups[1])
+    rows, width = kept.shape[0] // count, kept.shape[1]
+    pieces = {}
+    for first, last in ((count // 2, count), (0, count // 2)):
+        got = exchange(sent[first * rows : last * rows], groups[0][0])
+        shapes = [held(b16(rows, width) if block else f32(rows, width)) for block in range(first, last)]
+        sums = call(functools.partial(add_kernel, first * rows), shapes, Held(kept), Held(got))
+        pieces.update({block: total.array for block, total in zip(range(first, last), sums)})
+    gots = [send_block(pieces[block], groups[1], block) for block in range(count - 1, 0, -1)]
+    total = sum((got.astype(jnp.float32) for got in gots), pieces[0])
+    rows = total.shape[0] >> len(groups[2])
+    blocks = sorted(range(1, 1 << len(groups[2])), key=lambda block: (block != 2, block))
+    gots = [send_block(total[block * rows : (block + 1) * rows], groups[2], block) for block in blocks]
     attend_grad, output_grad = call(
         functools.partial(finish_kernel, split),
         (f32(rows * split // LANES, LANES), f32(rows * channels // LANES, LANES)),

time: 37.2 us -> 36.2 us (0.973)
  waiting for transfers between devices: 9.58 us -> 8.24 us
  starting transfers between devices: 13.2 us -> 13.7 us
    ppermute x7 -> x8, waiting for transfers between devices: 7.68 us -> 6.55 us  [exchange(): lax.ppermute(block, ('azim', 'frame'), [(i, i ^ mask) for i in range(memb...]
    ppermute x7 -> x8, starting transfers between devices: 8.08 us -> 8.64 us  [exchange(): lax.ppermute(block, ('azim', 'frame'), [(i, i ^ mask) for i in range(memb...]
    pallas_call x7 -> x9, Pallas kernels: 13.3 us -> 13.2 us  [call(): pl.pallas_call(body, out_shape=[space(m)(getattr(m, 'array', m).shape, ge...]
  transfers between devices with their start and end apart: 9 -> 10, of which waited for: 7 -> 6; matrix products, arithmetic and copies ran while one was open for 0% -> 0% of each run, Pallas kernels for 16% -> 17%
where the time goes in v2:
time: 36.2 us; the launch traced here: 36 us
  starting transfers between devices  13.7 us (38%)
  Pallas kernels  13.2 us (36%)
  waiting for transfers between devices  8.24 us (23%)
  between operations  0.73 us (2%)
    pallas_call x9, Pallas kernels, call(): pl.pallas_call(body, out_shape=[space(m)(getattr(m, 'array', m).shape, ge...  13.2 us
    ppermute x8, starting transfers between devices, exchange(): lax.ppermute(block, ('azim', 'frame'), [(i, i ^ mask) for i in range(memb...  8.64 us
    ppermute x8, waiting for transfers between devices, exchange(): lax.ppermute(block, ('azim', 'frame'), [(i, i ^ mask) for i in range(memb...  6.55 us
    ppermute x2, starting transfers between devices, from_behind(): lax.ppermute(block, axis, [((i - distance) % size, i) for i in range(size)])  5.09 us
    ppermute x2, waiting for transfers between devices, from_behind(): lax.ppermute(block, axis, [((i - distance) % size, i) for i in range(size)])  1.69 us
  transfers between devices with their start and end apart: 10, of which 6 were waited for; matrix products, arithmetic and copies ran while one was open for 0% of the time, Pallas kernels for 17%

profile of v2, /device:TPU:0, one launch (start us, length us, event | category | flops | bytes accessed | tf_op | source)
XLA Modules:
  0.0 36.0 jit_solution(3536658190202039056)
XLA Ops:
  0.6 1.3 %shard_map.192 = bf16[88,384]{1,0:T(8,128)(2,1)S(1)} custom-call(bf16[14,14,384]{2,1,0:T(8,128)(2,1)} %bitcast.7, bf16[7,7,768]{2,1,0:T(8,128)(2,1)} %bitcast.9, bf16[56,224]{1,0:T(8,128)(2,1)} %constant.21.clone.refs_2_, bf16[16,112]{1,0:T(8,128)(2,1)} %constant.22.clone.refs_3_), custom_call_target="tpu_custom_call" | custom-call | tf_op jit(solution)/shard_map/pallas_call | solution.py:568
  2.0 3.0 %collective-permute-start = (bf16[88,384]{1,0:T(8,128)(2,1)S(1)}, bf16[88,384]{1,0:T(8,128)(2,1)S(1)}, u32[]{:S(2)}, u32[]{:S(2)}) collective-permute-start(bf16[88,384]{1,0:T(8,128)(2,1)S(1)} %shard_map.192), channel_id=1, source_target_pairs={{28,0},{0,4},{4,8},{8,12},{12,16},{16,20},{20,24},{24,28},{29,1},{... | collective-permute-start | bytes 202760 | tf_op jit(solution)/shard_map/ppermute | solution.py:700
  5.0 3.6 %shard_map.193 = (bf16[256,280]{1,0:T(8,128)(2,1)S(1)}, bf16[384,1152]{1,0:T(8,128)(2,1)S(1)}, bf16[256,128]{1,0:T(8,128)(2,1)S(1)}, bf16[1536,768]{1,0:T(8,128)...) custom-call(bf16[14,14,384]{2,1,0:T(8,128)(2,1)} %bitcast.8, ...), custom_call_target="tpu_custom_call" | custom-call | tf_op jit(solution)/shard_map/pallas_call | solution.py:568
  8.6 1.7 %collective-permute-done.refs_0_ = bf16[88,384]{1,0:T(8,128)(2,1)S(1)} collective-permute-done((bf16[88,384]{1,0:T(8,128)(2,1)S(1)}, bf16[88,384]{1,0:T(8,128)(2,1)S(1)}, u32[]{:S(2)}, u32[]{:S(2)}) %collective-permute-start) | collective-permute-done | bytes 67616 | tf_op jit(solution)/shard_map/ppermute | solution.py:700
  10.3 5.1 %shard_map.194 = (f32[192,1536]{1,0:T(8,128)S(1)}, bf16[192,1536]{1,0:T(8,128)(2,1)S(1)}, bf16[256,1152]{1,0:T(8,128)(2,1)S(1)}, f32[256,384]{1,0:T(8,128)S(1)},...) custom-call(bf16[88,384]{1,0:T(8,128)(2,1)S(1)} %collective-permute-done.refs_0_, ...), custom_call_target="tpu_custom_call" | custom-call | tf_op jit(solution)/shard_map/pallas_call | solution.py:568
  15.5 0.1 collective-permute-start.3
  15.6 0.5 %collective-permute-start.2 = (bf16[96,1536]{1,0:T(8,128)(2,1)S(1)}, bf16[96,1536]{1,0:T(8,128)(2,1)S(1)}, u32[]{:S(2)}, u32[]{:S(2)}) collective-permute-start(bf16[96,1536]{1,0:T(8,128)(2,1)S(1)} %get-tuple-element.89), channel_id=1, source_target_pairs={{0,1},{1,0},{2,3},{3,2},{4,5},{5,4},{6,7},{7,6},{8,9},{9,8},{10,11... | collective-permute-start | bytes 884744 | tf_op jit(solution)/shard_map/ppermute | solution.py:605
  16.1 1.1 %collective-permute-done.3.refs_1_ = bf16[96,1536]{1,0:T(8,128)(2,1)S(1)} collective-permute-done((bf16[96,1536]{1,0:T(8,128)(2,1)S(1)}, bf16[96,1536]{1,0:T(8,128)(2,1)S(1)}, u32[]{:S(2)}, u32[]{:S(2)}) %collective-permute-start.3) | collective-permute-done | bytes 294944 | tf_op jit(solution)/shard_map/ppermute | solution.py:605
  17.1 0.1 shard_map.199
  17.2 0.9 %collective-permute-start.4 = (bf16[48,1536]{1,0:T(8,128)(2,1)S(1)}, bf16[48,1536]{1,0:T(8,128)(2,1)S(1)}, u32[]{:S(2)}, u32[]{:S(2)}) collective-permute-start(bf16[48,1536]{1,0:T(8,128)(2,1)S(1)} %get-tuple-element.81), channel_id=1, source_target_pairs={{0,6},{1,7},{2,4},{3,5},{4,2},{5,3},{6,0},{7,1},{8,14},{9,15},{10,... | collective-permute-start | bytes 442376 | tf_op jit(solution)/shard_map/ppermute | solution.py:605
  18.1 2.3 %collective-permute-start.5 = (bf16[48,1536]{1,0:T(8,128)(2,1)S(1)}, bf16[48,1536]{1,0:T(8,128)(2,1)S(1)}, u32[]{:S(2)}, u32[]{:S(2)}) collective-permute-start(bf16[48,1536]{1,0:T(8,128)(2,1)S(1)} %get-tuple-element.82), channel_id=1, source_target_pairs={{0,4},{1,5},{2,6},{3,7},{4,0},{5,1},{6,2},{7,3},{8,12},{9,13},{10,... | collective-permute-start | bytes 442376 | tf_op jit(solution)/shard_map/ppermute | solution.py:605
  20.4 0.0 collective-permute-done.2.refs_1_
  20.4 0.1 shard_map.198
  20.5 0.4 %collective-permute-start.6 = (bf16[48,1536]{1,0:T(8,128)(2,1)S(1)}, bf16[48,1536]{1,0:T(8,128)(2,1)S(1)}, u32[]{:S(2)}, u32[]{:S(2)}) collective-permute-start(bf16[48,1536]{1,0:T(8,128)(2,1)S(1)} %get-tuple-element.83), channel_id=1, source_target_pairs={{0,2},{1,3},{2,0},{3,1},{4,6},{5,7},{6,4},{7,5},{8,10},{9,11},{10,... | collective-permute-start | bytes 442376 | tf_op jit(solution)/shard_map/ppermute | solution.py:605
  20.9 0.5 %shard_map.195.refs_7_.refs_1_ = bf16[64,768]{1,0:T(8,128)(2,1)S(1)} custom-call(bf16[256,384]{1,0:T(8,128)(2,1)S(1)} %get-tuple-element.71.refs_0_, bf16[1536,768]{1,0:T(8,128)(2,1)S(1)} %get-tuple-element.53.refs_9_.refs_1_), custom_call_target="tpu_custom_call" | custom-call | tf_op jit(solution)/shard_map/pallas_call | solution.py:568
  21.4 0.8 %shard_map.196 = (bf16[88,384]{1,0:T(8,128)(2,1)S(1)}, bf16[256,384]{1,0:T(8,128)(2,1)S(1)}) custom-call(bf16[256,1152]{1,0:T(8,128)(2,1)S(1)} %get-tuple-element.65.refs_0_, bf16[384,1152]{1,0:T(8,128)(2,1)S(1)} %get-tuple-element.46.refs_2_.refs_1_, f32[256,384]{1,0:T(8,128)S(1)} %get-tuple-element.66.refs_2_, f32[256,1]{1,0:T(8,128)S(1)} %get-tuple-element.67.refs_3_, ...), custom_call_target="tpu_custom_call" | custom-call | tf_op jit(solution)/shard_map/pallas_call | solution.py:568
  22.3 2.1 %collective-permute-start.1 = (bf16[88,384]{1,0:T(8,128)(2,1)S(1)}, bf16[88,384]{1,0:T(8,128)(2,1)S(1)}, u32[]{:S(2)}, u32[]{:S(2)}) collective-permute-start(bf16[88,384]{1,0:T(8,128)(2,1)S(1)} %get-tuple-element.73), channel_id=1, source_target_pairs={{4,0},{8,4},{12,8},{16,12},{20,16},{24,20},{28,24},{0,28},{5,1},{9... | collective-permute-start | bytes 202760 | tf_op jit(solution)/shard_map/ppermute | solution.py:700
  24.3 0.6 %collective-permute-done.4 = bf16[48,1536]{1,0:T(8,128)(2,1)S(1)} collective-permute-done((bf16[48,1536]{1,0:T(8,128)(2,1)S(1)}, bf16[48,1536]{1,0:T(8,128)(2,1)S(1)}, u32[]{:S(2)}, u32[]{:S(2)}) %collective-permute-start.4) | collective-permute-done | bytes 147488 | tf_op jit(solution)/shard_map/ppermute | solution.py:605
  24.9 3.3 %collective-permute-done.5 = bf16[48,1536]{1,0:T(8,128)(2,1)S(1)} collective-permute-done((bf16[48,1536]{1,0:T(8,128)(2,1)S(1)}, bf16[48,1536]{1,0:T(8,128)(2,1)S(1)}, u32[]{:S(2)}, u32[]{:S(2)}) %collective-permute-start.5) | collective-permute-done | bytes 147488 | tf_op jit(solution)/shard_map/ppermute | solution.py:605
  28.2 0.0 collective-permute-done.6
  28.2 0.1 fusion
  28.4 1.9 %collective-permute-start.9 = (bf16[12,1536]{1,0:T(8,128)(2,1)S(1)}, bf16[12,1536]{1,0:T(8,128)(2,1)S(1)}, u32[]{:S(2)}, u32[]{:S(2)}) collective-permute-start(bf16[12,1536]{1,0:T(8,128)(2,1)S(1)} %get-tuple-element.90), channel_id=1, source_target_pairs={{0,24},{1,25},{2,26},{3,27},{4,28},{5,29},{6,30},{7,31},{8,16},{9,... | collective-permute-start | bytes 110600 | tf_op jit(solution)/shard_map/ppermute | solution.py:605
  30.2 0.0 collective-permute-start.8
  30.2 2.6 %collective-permute-start.7 = (bf16[12,1536]{1,0:T(8,128)(2,1)S(1)}, bf16[12,1536]{1,0:T(8,128)(2,1)S(1)}, u32[]{:S(2)}, u32[]{:S(2)}) collective-permute-start(bf16[12,1536]{1,0:T(8,128)(2,1)S(1)} %get-tuple-element.92), channel_id=1, source_target_pairs={{0,16},{1,17},{2,18},{3,19},{4,20},{5,21},{6,22},{7,23},{8,24},{9,... | collective-permute-start | bytes 110600 | tf_op jit(solution)/shard_map/ppermute | solution.py:605
  32.8 0.0 collective-permute-done.1.refs_2_
  32.8 1.0 %shard_map.197 = (bf16[14,14,384]{2,1,0:T(8,128)(2,1)}, bf16[7,7,768]{2,1,0:T(8,128)(2,1)}) custom-call(bf16[256,384]{1,0:T(8,128)(2,1)S(1)} %get-tuple-element.72.refs_0_, bf16[64,768]{1,0:T(8,128)(2,1)S(1)} %shard_map.195.refs_7_.refs_1_, bf16[88,384]{1,0:T(8,128)(2,1)S(1)} %collective-permute-done.1.refs_2_, ...), custom_call_target="tpu_custom_call" | custom-call | tf_op jit(solution)/shard_map/pallas_call | solution.py:568
  33.8 0.9 %collective-permute-done.9.refs_3_ = bf16[12,1536]{1,0:T(8,128)(2,1)S(1)} collective-permute-done((bf16[12,1536]{1,0:T(8,128)(2,1)S(1)}, bf16[12,1536]{1,0:T(8,128)(2,1)S(1)}, u32[]{:S(2)}, u32[]{:S(2)}) %collective-permute-start.9) | collective-permute-done | bytes 36896 | tf_op jit(solution)/shard_map/ppermute | solution.py:605
  34.7 0.6 %collective-permute-done.8.refs_2_ = bf16[12,1536]{1,0:T(8,128)(2,1)S(1)} collective-permute-done((bf16[12,1536]{1,0:T(8,128)(2,1)S(1)}, bf16[12,1536]{1,0:T(8,128)(2,1)S(1)}, u32[]{:S(2)}, u32[]{:S(2)}) %collective-permute-start.8) | collective-permute-done | bytes 36896 | tf_op jit(solution)/shard_map/ppermute | solution.py:605
  35.4 0.0 collective-permute-done.7.refs_1_
  35.4 0.7 %shard_map.200 = (f32[108,128]{1,0:T(8,128)}, f32[36,128]{1,0:T(8,128)}) custom-call(f32[48,1536]{1,0:T(8,128)S(1)} %get-tuple-element.87.refs_0_, bf16[12,1536]{1,0:T(8,128)(2,1)S(1)} %collective-permute-done.7.refs_1_, bf16[12,1536]{1,0:T(8,128)(2,1)S(1)} %collective-permute-done.8.refs_2_, bf16[12,1536]{1,0:T(8,128)(2,1)S(1)} %collective-permute-done.9.refs_3_), custom_call_target="tpu_custom_call" | custom-call | tf_op jit(solution)/shard_map/pallas_call | solution.py:568
  (2 shorter events, 0.1 us)
Async XLA Ops:
  2.0 8.3 %collective-permute-start = (bf16[88,384]{1,0:T(8,128)(2,1)S(1)}, bf16[88,384]{1,0:T(8,128)(2,1)S(1)}, u32[]{:S(2)}, u32[]{:S(2)}) collective-permute-start(bf16[88,384]{1,0:T(8,128)(2,1)S(1)} %shard_map.192), channel_id=1, source_target_pairs={{28,0},{0,4},{4,8},{8,12},{12,16},{16,20},{20,24},{24,28},{29,1},{... | collective-permute-start | bytes 202760 | tf_op jit(solution)/shard_map/ppermute | solution.py:700
  15.5 1.6 %collective-permute-start.3 = (bf16[96,1536]{1,0:T(8,128)(2,1)S(1)}, bf16[96,1536]{1,0:T(8,128)(2,1)S(1)}, u32[]{:S(2)}, u32[]{:S(2)}) collective-permute-start(bf16[96,1536]{1,0:T(8,128)(2,1)S(1)} %get-tuple-element.88), channel_id=1, source_target_pairs={{0,1},{1,0},{2,3},{3,2},{4,5},{5,4},{6,7},{7,6},{8,9},{9,8},{10,11... | collective-permute-start | bytes 884744 | tf_op jit(solution)/shard_map/ppermute | solution.py:605
  15.6 4.9 %collective-permute-start.2 = (bf16[96,1536]{1,0:T(8,128)(2,1)S(1)}, bf16[96,1536]{1,0:T(8,128)(2,1)S(1)}, u32[]{:S(2)}, u32[]{:S(2)}) collective-permute-start(bf16[96,1536]{1,0:T(8,128)(2,1)S(1)} %get-tuple-element.89), channel_id=1, source_target_pairs={{0,1},{1,0},{2,3},{3,2},{4,5},{5,4},{6,7},{7,6},{8,9},{9,8},{10,11... | collective-permute-start | bytes 884744 | tf_op jit(solution)/shard_map/ppermute | solution.py:605
  17.2 7.7 %collective-permute-start.4 = (bf16[48,1536]{1,0:T(8,128)(2,1)S(1)}, bf16[48,1536]{1,0:T(8,128)(2,1)S(1)}, u32[]{:S(2)}, u32[]{:S(2)}) collective-permute-start(bf16[48,1536]{1,0:T(8,128)(2,1)S(1)} %get-tuple-element.81), channel_id=1, source_target_pairs={{0,6},{1,7},{2,4},{3,5},{4,2},{5,3},{6,0},{7,1},{8,14},{9,15},{10,... | collective-permute-start | bytes 442376 | tf_op jit(solution)/shard_map/ppermute | solution.py:605
  18.1 10.1 %collective-permute-start.5 = (bf16[48,1536]{1,0:T(8,128)(2,1)S(1)}, bf16[48,1536]{1,0:T(8,128)(2,1)S(1)}, u32[]{:S(2)}, u32[]{:S(2)}) collective-permute-start(bf16[48,1536]{1,0:T(8,128)(2,1)S(1)} %get-tuple-element.82), channel_id=1, source_target_pairs={{0,4},{1,5},{2,6},{3,7},{4,0},{5,1},{6,2},{7,3},{8,12},{9,13},{10,... | collective-permute-start | bytes 442376 | tf_op jit(solution)/shard_map/ppermute | solution.py:605
  20.5 7.7 %collective-permute-start.6 = (bf16[48,1536]{1,0:T(8,128)(2,1)S(1)}, bf16[48,1536]{1,0:T(8,128)(2,1)S(1)}, u32[]{:S(2)}, u32[]{:S(2)}) collective-permute-start(bf16[48,1536]{1,0:T(8,128)(2,1)S(1)} %get-tuple-element.83), channel_id=1, source_target_pairs={{0,2},{1,3},{2,0},{3,1},{4,6},{5,7},{6,4},{7,5},{8,10},{9,11},{10,... | collective-permute-start | bytes 442376 | tf_op jit(solution)/shard_map/ppermute | solution.py:605
  22.3 10.6 %collective-permute-start.1 = (bf16[88,384]{1,0:T(8,128)(2,1)S(1)}, bf16[88,384]{1,0:T(8,128)(2,1)S(1)}, u32[]{:S(2)}, u32[]{:S(2)}) collective-permute-start(bf16[88,384]{1,0:T(8,128)(2,1)S(1)} %get-tuple-element.73), channel_id=1, source_target_pairs={{4,0},{8,4},{12,8},{16,12},{20,16},{24,20},{28,24},{0,28},{5,1},{9... | collective-permute-start | bytes 202760 | tf_op jit(solution)/shard_map/ppermute | solution.py:700
  28.4 6.3 %collective-permute-start.9 = (bf16[12,1536]{1,0:T(8,128)(2,1)S(1)}, bf16[12,1536]{1,0:T(8,128)(2,1)S(1)}, u32[]{:S(2)}, u32[]{:S(2)}) collective-permute-start(bf16[12,1536]{1,0:T(8,128)(2,1)S(1)} %get-tuple-element.90), channel_id=1, source_target_pairs={{0,24},{1,25},{2,26},{3,27},{4,28},{5,29},{6,30},{7,31},{8,16},{9,... | collective-permute-start | bytes 110600 | tf_op jit(solution)/shard_map/ppermute | solution.py:605
  30.2 5.1 %collective-permute-start.8 = (bf16[12,1536]{1,0:T(8,128)(2,1)S(1)}, bf16[12,1536]{1,0:T(8,128)(2,1)S(1)}, u32[]{:S(2)}, u32[]{:S(2)}) collective-permute-start(bf16[12,1536]{1,0:T(8,128)(2,1)S(1)} %get-tuple-element.91), channel_id=1, source_target_pairs={{0,8},{1,9},{2,10},{3,11},{4,12},{5,13},{6,14},{7,15},{8,0},{9,1},... | collective-permute-start | bytes 110600 | tf_op jit(solution)/shard_map/ppermute | solution.py:605
  30.2 5.1 %collective-permute-start.7 = (bf16[12,1536]{1,0:T(8,128)(2,1)S(1)}, bf16[12,1536]{1,0:T(8,128)(2,1)S(1)}, u32[]{:S(2)}, u32[]{:S(2)}) collective-permute-start(bf16[12,1536]{1,0:T(8,128)(2,1)S(1)} %get-tuple-element.92), channel_id=1, source_target_pairs={{0,16},{1,17},{2,18},{3,19},{4,20},{5,21},{6,22},{7,23},{8,24},{9,... | collective-permute-start | bytes 110600 | tf_op jit(solution)/shard_map/ppermute | solution.py:605
